TPU v7x, 512 devices: a whole 4x4x16 slice. The times are simulated.
512 devices in a mesh: dp: 16 (over x_lo, y, core), vocab: 32 (over z, x_hi).
Axes of the slice: x: 4 (x_hi: 2, x_lo: 2; x = x_hi * 2 + x_lo), y: 4, z: 16, core: 2. Of those that a mesh axis runs over, the one named last changes fastest.
Arguments:
- passage_hidden: bfloat16 [2048, 2048], P('dp'), may hold values from -7 to 7
- passage_lengths: int32 [32], P('dp'), may hold values from 16 to 64, as said below
- query_ids: int32 [32, 16], P('dp'), may hold values from 0 to 131071
- query_lengths: int32 [32], P('dp'), may hold values from 4 to 16, as said below
- positives: int32 [32], replicated, may hold values from 0 to 31, each once
- head: bfloat16 [2048, 131072], P('dp', 'vocab'), may hold values from -0.125 to 0.125
- df_prev: float32 [131072], P('vocab'), may hold values from 1 to 4096
Outputs:
- head_grad: float32 [2048, 131072], P('dp', 'vocab')
- scores: float32 [32, 32], replicated
Inputs may be any that keep to these rules, and one draw needn't show every extreme that they name: `passage_lengths`: some passage fills all 64 slots. `query_lengths`: some query fills all 16 slots. `positives`: each passage is the positive of exactly one query.
All inputs are finite; a program needn't handle non-finite values.
Results may differ from a plain program's by a relative error of at most 0.00064.
Values may be sent and summed in bfloat16 or wider, within the bound.
No kernel may reach another device: no remote copies, remote signals or barrier semaphores. Data moves between devices by JAX's collectives and lax.ppermute only.
A program may use at most 64 MiB of HBM per device.

v0:
```python
import jax
import jax.numpy as jnp
from jax import lax
from jax.sharding import Mesh, PartitionSpec as P

flops_weight = 0.3
DP = ("xl", "y", "c")
VOCAB = ("z", "xh")
PLANE = ("xl", "y", "c", "xh")


def ranking_grad(scores, chosen, query_total):
    columns = scores.shape[1]
    onehot = (jnp.arange(columns, dtype=jnp.int32)[None, :] == chosen[:, None]).astype(jnp.float32)
    own_score = jnp.sum(scores * onehot, axis=1, keepdims=True)
    sigmas = jax.nn.sigmoid(scores - own_score)
    return (sigmas - onehot * jnp.sum(sigmas, axis=1, keepdims=True)) / query_total


def spread(value, axes):
    count = lax.axis_size(axes)
    return lax.all_to_all(
        jnp.broadcast_to(value[None], (count,) + value.shape), axes, 0, 0, tiled=True
    )


def local(passage_hidden, passage_lengths, query_ids, query_lengths, positives, head, df_prev):
    dp_count = lax.axis_size(DP)
    dp_index = lax.axis_index(DP)
    vocab_index = lax.axis_index(VOCAB)
    width_local = head.shape[1]
    column_count = width_local // dp_count
    query_slots = query_ids.shape[1]
    packed = jnp.concatenate([query_ids, query_lengths[:, None], passage_lengths[:, None]], axis=1)
    packed = spread(packed, DP).reshape(-1, query_slots + 2)
    query_tokens = packed[:, :query_slots]
    query_sizes = packed[:, query_slots]
    passage_sizes = packed[:, query_slots + 1]
    head_block = lax.all_to_all(head, DP, split_axis=1, concat_axis=0, tiled=True)
    hidden_all = lax.all_gather(passage_hidden, DP, axis=0, tiled=True)
    passage_count = passage_sizes.shape[0]
    seq_span = hidden_all.shape[0] // passage_count
    logits = jnp.dot(hidden_all, head_block, preferred_element_type=jnp.float32)
    softened = jax.nn.softplus(logits)
    activation = jnp.log1p(softened)
    slope_term = jax.nn.sigmoid(logits) / (1.0 + softened)
    positions = jnp.arange(seq_span, dtype=jnp.int32)
    token_mask = (positions[None, :] < passage_sizes[:, None]).astype(jnp.float32)
    token_weight = token_mask / passage_sizes.astype(jnp.float32)[:, None]
    passage_rep = jnp.sum(
        activation.reshape(passage_count, seq_span, column_count) * token_weight[:, :, None], axis=1
    )
    first_column = dp_index * column_count
    doc_freq = lax.dynamic_slice_in_dim(df_prev, first_column, column_count, 0) + jnp.sum(
        1.0 - jnp.exp(-2.0 * passage_rep), axis=0
    )
    term_weight = jnp.log1p(doc_freq)
    column_ids = (
        vocab_index * width_local + first_column + jnp.arange(column_count, dtype=jnp.int32)
    )
    query_mask = jnp.arange(query_slots, dtype=jnp.int32)[None, :] < query_sizes[:, None]
    matches = (query_tokens[:, :, None] == column_ids[None, None, :]) & query_mask[:, :, None]
    query_bag = jnp.sum(matches.astype(jnp.float32), axis=1)
    partial_scores = jnp.dot(
        query_bag,
        passage_rep.T,
        precision=lax.Precision.HIGHEST,
        preferred_element_type=jnp.float32,
    )
    query_total = positives.shape[0]
    plane_scores = jnp.sum(spread(partial_scores, PLANE), axis=0)
    scores = jnp.sum(spread(plane_scores, "z"), axis=0)
    score_grad = ranking_grad(scores, positives, query_total)
    rep_grad = jnp.dot(
        score_grad.T, query_bag, precision=lax.Precision.HIGHEST, preferred_element_type=jnp.float32
    )
    rep_grad = rep_grad + 2.0 * flops_weight / passage_count * term_weight * jnp.mean(
        passage_rep, axis=0
    )
    logit_grad = (
        (token_weight[:, :, None] * rep_grad[:, None, :]).reshape(logits.shape) * slope_term
    ).astype(jnp.bfloat16)
    grad_block = lax.dot_general(
        hidden_all, logit_grad, (((0,), (0,)), ((), ())), preferred_element_type=jnp.float32
    )
    head_grad = lax.all_to_all(grad_block, DP, split_axis=0, concat_axis=1, tiled=True)
    return (head_grad, scores)


def solution(mesh):
    fine = Mesh(mesh.devices.reshape(2, 4, 2, 16, 2), DP + VOCAB)
    return jax.shard_map(
        local,
        mesh=fine,
        in_specs=(P(DP, None), P(DP), P(DP, None), P(DP), P(), P(DP, VOCAB), P(VOCAB)),
        out_specs=(P(DP, VOCAB), P()),
        check_vma=False,
    )
```

profile of v0, /device:TPU:1, one launch (start us, length us, event | category | flops | bytes accessed | tf_op | source)
XLA Modules:
  0.0 185.7 jit_solution(16136462028311963725)
XLA Ops:
  7.2 0.7 all-gather.2.cloned.1.call-update
  7.9 0.7 copy.29
  8.6 0.7 copy.28
  9.4 0.8 pad_add_fusion
  10.1 0.6 broadcast_in_dim.12
  10.7 10.1 %all-to-all-start = ((s32[16,2,18]{2,1,0:T(2,128)}), s32[16,2,18]{2,1,0:T(2,128)S(1)}, u32[]{:S(2)}, u32[]{:S(2)}) async-start(s32[16,2,18]{2,1,0:T(2,128)} %broadcast_in_dim.12), calls=%async_computation | async-start | bytes 32768 | tf_op jit(solution)/shard_map/all_to_all | solution.py:22
  20.9 2.3 %copy.30 = bf16[128,4096]{0,1:T(8,128)(2,1)} copy(bf16[128,4096]{1,0:T(8,128)(2,1)} %param.12) | data formatting | bytes 2097152 | tf_op args[5]
  23.1 3.6 %all-to-all-done = s32[16,2,18]{2,1,0:T(2,128)S(1)} async-done(((s32[16,2,18]{2,1,0:T(2,128)}), s32[16,2,18]{2,1,0:T(2,128)S(1)}, u32[]{:S(2)}, u32[]{:S(2)}) %all-to-all-start) | async-done | bytes 2336 | tf_op jit(solution)/shard_map/all_to_all | solution.py:22
  26.7 3.8 %all-to-all-start.1 = ((bf16[128,16,256]{0,2,1:T(8,128)(2,1)}), bf16[128,16,256]{0,2,1:T(8,128)(2,1)S(1)}, u32[]{:S(2)}, u32[]{:S(2)}) async-start(bf16[128,16,256]{0,2,1:T(8,128)(2,1)} %bitcast.3), calls=%async_computation.1 | async-start | bytes 2097152 | tf_op jit(solution)/shard_map/all_to_all | solution.py:39
  31.2 0.3 convert_reduce_fusion
  31.4 24.5 %all-to-all-done.1 = bf16[128,16,256]{0,2,1:T(8,128)(2,1)S(1)} async-done(((bf16[128,16,256]{0,2,1:T(8,128)(2,1)}), bf16[128,16,256]{0,2,1:T(8,128)(2,1)S(1)}, u32[]{:S(2)}, u32[]{:S(2)}) %all-to-all-start.1) | async-done | bytes 1048608 | tf_op jit(solution)/shard_map/all_to_all | solution.py:39
  55.9 0.5 copy.31
  56.5 29.3 %all-gather.2.cloned.1.call-done = bf16[2048,2048]{1,0:T(8,128)(2,1)} async-done(((bf16[128,2048]{1,0:T(8,128)(2,1)}), bf16[2048,2048]{1,0:T(8,128)(2,1)}) %all-gather.2.cloned.1.call-update) | async-done | bytes 8388624 | tf_op jit(solution)/shard_map/all_gather | solution.py:40
  85.7 7.4 %multiply_reduce_fusion = (f32[256]{0:T(256)S(1)}, f32[2048,256]{1,0:T(8,128)S(1)}) fusion(f32[2048]{0:T(1024)S(1)} %div.40, bf16[2048,2048]{1,0:T(8,128)(2,1)} %all-gather.2.cloned.1.call-done, bf16[2048,256]{1,0:T(8,128)(2,1)S(1)} %bitcast.34), kind=kOutput, calls=%fused_computation.5 | convolution fusion | flops 2151677696 | bytes 11543552 | tf_op jit(solution)/shard_map/dot_general | solution.py:43
  93.1 1.9 %multiply_reduce_fusion.1 = f32[32,256]{1,0:T(8,128)S(1)} fusion(f32[32,64]{1,0:T(8,128)S(1)} %convert_divide_fusion, f32[2048,256]{1,0:T(8,128)S(1)} %get-tuple-element.9), kind=kLoop, calls=%fused_computation.6 | loop fusion | flops 4186112 | bytes 2138112 | tf_op jit(solution)/shard_map/reduce_sum | solution.py:50
  95.3 0.9 reshape.108
  96.2 5.2 %all-to-all-start.2 = ((f32[32,1,1024]{2,1,0:T(1,128)}), f32[32,1,1024]{2,1,0:T(1,128)S(1)}, u32[]{:S(2)}, u32[]{:S(2)}) async-start(f32[32,1,1024]{2,1,0:T(1,128)} %reshape.108), calls=%async_computation.2 | async-start | bytes 262144 | tf_op jit(solution)/shard_map/all_to_all | solution.py:22
  101.4 7.7 %all-to-all-done.2 = f32[32,1,1024]{2,1,0:T(1,128)S(1)} async-done(((f32[32,1,1024]{2,1,0:T(1,128)}), f32[32,1,1024]{2,1,0:T(1,128)S(1)}, u32[]{:S(2)}, u32[]{:S(2)}) %all-to-all-start.2) | async-done | bytes 131104 | tf_op jit(solution)/shard_map/all_to_all | solution.py:22
  109.1 0.5 broadcast.88
  109.6 0.9 reduce.8
  110.8 0.8 reshape.110
  111.6 13.1 %all-to-all-start.3 = ((f32[16,1,1024]{2,1,0:T(1,128)}), f32[16,1,1024]{2,1,0:T(1,128)S(1)}, u32[]{:S(2)}, u32[]{:S(2)}) async-start(f32[16,1,1024]{2,1,0:T(1,128)} %reshape.110), calls=%async_computation.3 | async-start | bytes 131072 | tf_op jit(solution)/shard_map/all_to_all | solution.py:22
  124.8 0.8 multiply_multiply_fusion
  125.5 10.8 %all-to-all-done.3 = f32[16,1,1024]{2,1,0:T(1,128)S(1)} async-done(((f32[16,1,1024]{2,1,0:T(1,128)}), f32[16,1,1024]{2,1,0:T(1,128)S(1)}, u32[]{:S(2)}, u32[]{:S(2)}) %all-to-all-start.3) | async-done | bytes 65568 | tf_op jit(solution)/shard_map/all_to_all | solution.py:22
  136.3 0.8 reduce.9
  137.5 0.2 fusion.12
  137.6 0.3 convolution_add_fusion
  138.0 1.7 fusion.1
  139.7 5.7 %convolution_bitcast_fusion = f32[32,16,8,128]{3,2,1,0:T(8,128)S(1)} fusion(bf16[2048,256]{1,0:T(8,128)(2,1)S(1)} %fusion.1, bf16[2048,2048]{1,0:T(8,128)(2,1)} %all-gather.2.cloned.1.call-done), kind=kOutput, calls=%fused_computation.8 | convolution fusion | flops 2147483648 | bytes 11534336 | tf_op jit(solution)/shard_map/dot_general | solution.py:83
  145.5 0.2 copy.36
  145.7 31.3 %all_to_all.53 = f32[16,128,256]{1,2,0:T(8,128)S(1)} all-to-all(f32[16,128,256]{1,2,0:T(8,128)S(1)} %bitcast.31), channel_id=1, replica_groups=mesh['xl'=2,'y'=4,'c'=2,'z'=16,'xh'=2] {'xl','y','c'}, dimensions={0} | all-to-all | bytes 4194304 | tf_op jit(solution)/shard_map/all_to_all | solution.py:86
  177.0 1.8 copy.33
  (20 shorter events, 1.4 us)
Async XLA Ops:
  7.2 78.6 %all-gather.2.cloned.1.call-start = ((), (), s32[]{:S(2)}) async-start(), calls=%async_computation.5 | async-start | bytes 8912896 | tf_op jit(solution)/shard_map/all_gather | solution.py:40
  10.7 16.0 %all-to-all-start = ((s32[16,2,18]{2,1,0:T(2,128)}), s32[16,2,18]{2,1,0:T(2,128)S(1)}, u32[]{:S(2)}, u32[]{:S(2)}) async-start(s32[16,2,18]{2,1,0:T(2,128)} %broadcast_in_dim.12), calls=%async_computation | async-start | bytes 32768 | tf_op jit(solution)/shard_map/all_to_all | solution.py:22
  26.7 29.2 %all-to-all-start.1 = ((bf16[128,16,256]{0,2,1:T(8,128)(2,1)}), bf16[128,16,256]{0,2,1:T(8,128)(2,1)S(1)}, u32[]{:S(2)}, u32[]{:S(2)}) async-start(bf16[128,16,256]{0,2,1:T(8,128)(2,1)} %bitcast.3), calls=%async_computation.1 | async-start | bytes 2097152 | tf_op jit(solution)/shard_map/all_to_all | solution.py:39
  95.2 42.0 %copy-start.1 = (s32[32]{0:T(128)S(1)}, s32[32]{0:T(128)}, u32[]{:S(2)}) copy-start(s32[32]{0:T(128)} %param.11) | copy-start | bytes 388
  96.2 12.9 %all-to-all-start.2 = ((f32[32,1,1024]{2,1,0:T(1,128)}), f32[32,1,1024]{2,1,0:T(1,128)S(1)}, u32[]{:S(2)}, u32[]{:S(2)}) async-start(f32[32,1,1024]{2,1,0:T(1,128)} %reshape.108), calls=%async_computation.2 | async-start | bytes 262144 | tf_op jit(solution)/shard_map/all_to_all | solution.py:22
  111.6 24.7 %all-to-all-start.3 = ((f32[16,1,1024]{2,1,0:T(1,128)}), f32[16,1,1024]{2,1,0:T(1,128)S(1)}, u32[]{:S(2)}, u32[]{:S(2)}) async-start(f32[16,1,1024]{2,1,0:T(1,128)} %reshape.110), calls=%async_computation.3 | async-start | bytes 131072 | tf_op jit(solution)/shard_map/all_to_all | solution.py:22
  137.3 8.2 %copy-start = (f32[32,32]{1,0:T(8,128)}, f32[32,32]{1,0:T(8,128)S(1)}, u32[]{:S(2)}) copy-start(f32[32,32]{1,0:T(8,128)S(1)} %reduce_sum.75) | copy-start | bytes 12292
Sparse Core Ops, SparseCore 0:
  10.1 75.5 all-gather.1
where the time goes:
time: 186 us
  waiting for transfers between devices  76.5 us (41%)
  starting transfers between devices  32.3 us (17%)
  blocking collectives  31.3 us (17%)
  between operations  14.2 us (8%)
  matrix products  13.6 us (7%)
  local copies, waits for them, and re-layouts  9.72 us (5%)
  other arithmetic  8.02 us (4%)
    all_to_all x1, blocking collectives, local(): lax.all_to_all(grad_block, DP, split_axis=0, concat_axis=1, tiled=True)  31.3 us
    all_gather x1, waiting for transfers between devices, local(): hidden_all = lax.all_gather(passage_hidden, DP, axis=0, tiled=True)  29.3 us
    all_to_all x3, starting transfers between devices, spread(): lax.all_to_all(jnp.broadcast_to(value[None], (count,) + value.shape), axe...  28.4 us
    all_to_all x1, waiting for transfers between devices, local(): lax.all_to_all(head, DP, split_axis=1, concat_axis=0, tiled=True)  24.5 us
    all_to_all x3, waiting for transfers between devices, spread(): lax.all_to_all(jnp.broadcast_to(value[None], (count,) + value.shape), axe...  22 us
    dot_general x1, matrix products, local(): logits = jnp.dot(hidden_all, head_block, preferred_element_type=jnp.float32)  7.39 us
    unnamed x10, local copies, waits for them, and re-layouts  6.06 us
    dot_general x1, matrix products, local(): lax.dot_general(hidden_all, logit_grad, (((0,), (0,)), ((), ())), preferr...  5.74 us
  transfers between devices with their start and end apart: 5, of which 5 were waited for; matrix products, arithmetic and copies ran while one was open for 4% of the time, Pallas kernels for 0%

commit v1 on v0

--- a/solution.py
+++ b/solution.py
@@ -37,7 +37,14 @@
     query_sizes = packed[:, query_slots]
     passage_sizes = packed[:, query_slots + 1]
     head_block = lax.all_to_all(head, DP, split_axis=1, concat_axis=0, tiled=True)
-    hidden_all = lax.all_gather(passage_hidden, DP, axis=0, tiled=True)
+
+    def convert_paths(inputs, named_axis, which_dim):
+        high = jnp.stack([inputs for _ in range(jax.lax.axis_size(named_axis))])
+        taken_in = jax.lax.all_to_all(high, named_axis, 0, 0)
+        z2 = jnp.concatenate(taken_in, axis=which_dim)
+        return z2
+
+    hidden_all = convert_paths(passage_hidden, DP, 0)
     passage_count = passage_sizes.shape[0]
     seq_span = hidden_all.shape[0] // passage_count
     logits = jnp.dot(hidden_all, head_block, preferred_element_type=jnp.float32)

time: 186 us -> 269 us (1.45)
  waiting for transfers between devices: 76.5 us -> 142 us
  blocking collectives: 31.3 us -> 49.5 us
  between operations: 14.2 us -> 0.82 us
  starting transfers between devices: 32.3 us -> 40.8 us
  local copies, waits for them, and re-layouts: 9.72 us -> 13.4 us
    all_to_all x1, waiting for transfers between devices: 24.5 us -> 120 us  [convert_paths(): taken_in = jax.lax.all_to_all(high, named_axis, 0, 0)]
    all_gather x1 -> x0, waiting for transfers between devices: 29.3 us -> none  [local(): hidden_all = lax.all_gather(passage_hidden, DP, axis=0, tiled=True)]
    all_to_all x0 -> x1, blocking collectives: none -> 18.2 us  [local(): lax.all_to_all(head, DP, split_axis=1, concat_axis=0, tiled=True)]
    all_to_all x3, starting transfers between devices: 28.4 us -> 35.1 us  [spread(): lax.all_to_all(jnp.broadcast_to(value[None], (count,) + value.shape), axe...]
    another operation x0 -> x1, local copies, waits for them, and re-layouts: none -> 4.3 us  [convert_paths(): high = jnp.stack([inputs for _ in range(jax.lax.axis_size(named_axis))])]
    unnamed x10 -> x12, local copies, waits for them, and re-layouts: 6.06 us -> 5.48 us
  transfers between devices with their start and end apart: 5 -> 4, of which waited for: 5 -> 4; matrix products, arithmetic and copies ran while one was open for 4% -> 1% of each run, Pallas kernels for 0% -> 0%
where the time goes in v1:
time: 269 us
  waiting for transfers between devices  142 us (53%)
  blocking collectives  49.5 us (18%)
  starting transfers between devices  40.8 us (15%)
  matrix products  13.6 us (5%)
  local copies, waits for them, and re-layouts  13.4 us (5%)
  other arithmetic  8.02 us (3%)
    all_to_all x1, waiting for transfers between devices, convert_paths(): taken_in = jax.lax.all_to_all(high, named_axis, 0, 0)  120 us
    all_to_all x3, starting transfers between devices, spread(): lax.all_to_all(jnp.broadcast_to(value[None], (count,) + value.shape), axe...  35.1 us
    all_to_all x1, blocking collectives, local(): lax.all_to_all(grad_block, DP, split_axis=0, concat_axis=1, tiled=True)  31.3 us
    all_to_all x3, waiting for transfers between devices, spread(): lax.all_to_all(jnp.broadcast_to(value[None], (count,) + value.shape), axe...  22.6 us
    all_to_all x1, blocking collectives, local(): lax.all_to_all(head, DP, split_axis=1, concat_axis=0, tiled=True)  18.2 us
    dot_general x1, matrix products, local(): logits = jnp.dot(hidden_all, head_block, preferred_element_type=jnp.float32)  7.38 us
    dot_general x1, matrix products, local(): lax.dot_general(hidden_all, logit_grad, (((0,), (0,)), ((), ())), preferr...  5.74 us
    all_to_all x1, starting transfers between devices, convert_paths(): taken_in = jax.lax.all_to_all(high, named_axis, 0, 0)  5.72 us
  transfers between devices with their start and end apart: 4, of which 4 were waited for; matrix products, arithmetic and copies ran while one was open for 1% of the time, Pallas kernels for 0%

profile of v1, /device:TPU:1, one launch (start us, length us, event | category | flops | bytes accessed | tf_op | source)
XLA Modules:
  0.0 268.7 jit_solution(3497109382755291323)
XLA Ops:
  0.6 0.7 copy.29
  1.4 0.7 copy.28
  2.1 0.8 pad_add_fusion
  2.9 0.6 broadcast_in_dim.12
  3.5 10.1 %all-to-all-start = ((s32[16,2,18]{2,1,0:T(2,128)}), s32[16,2,18]{2,1,0:T(2,128)S(1)}, u32[]{:S(2)}, u32[]{:S(2)}) async-start(s32[16,2,18]{2,1,0:T(2,128)} %broadcast_in_dim.12), calls=%async_computation | async-start | bytes 32768 | tf_op jit(solution)/shard_map/all_to_all | solution.py:22
  13.6 1.7 copy.30
  15.3 4.2 %all-to-all-done = s32[16,2,18]{2,1,0:T(2,128)S(1)} async-done(((s32[16,2,18]{2,1,0:T(2,128)}), s32[16,2,18]{2,1,0:T(2,128)S(1)}, u32[]{:S(2)}, u32[]{:S(2)}) %all-to-all-start) | async-done | bytes 2336 | tf_op jit(solution)/shard_map/all_to_all | solution.py:22
  19.5 18.2 %all_to_all.58 = bf16[128,16,256]{0,2,1:T(8,128)(2,1)S(1)} all-to-all(bf16[128,16,256]{0,2,1:T(8,128)(2,1)S(1)} %bitcast.35), channel_id=1, replica_groups=mesh['xl'=2,'y'=4,'c'=2,'z'=16,'xh'=2] {'xl','y','c'}, dimensions={1} | all-to-all | bytes 2097152 | tf_op jit(solution)/shard_map/all_to_all | solution.py:39
  37.7 4.3 %stack.2 = bf16[16,128,2048]{2,1,0:T(8,128)(2,1)} broadcast(bf16[128,2048]{1,0:T(8,128)(2,1)S(1)} %copy-done), dimensions={1,2} | broadcast | bytes 8912896 | tf_op jit(solution)/shard_map/stack | solution.py:42
  42.0 5.7 %all-to-all-start.1 = ((bf16[16,128,2048]{2,1,0:T(8,128)(2,1)}), bf16[16,128,2048]{2,1,0:T(8,128)(2,1)}, u32[]{:S(2)}, u32[]{:S(2)}) async-start(bf16[16,128,2048]{2,1,0:T(8,128)(2,1)} %stack.2), calls=%async_computation.1 | async-start | bytes 16777216 | tf_op jit(solution)/shard_map/all_to_all | solution.py:43
  48.3 0.3 convert_reduce_fusion
  48.6 0.5 copy.31
  49.1 119.9 %all-to-all-done.1 = bf16[16,128,2048]{2,1,0:T(8,128)(2,1)} async-done(((bf16[16,128,2048]{2,1,0:T(8,128)(2,1)}), bf16[16,128,2048]{2,1,0:T(8,128)(2,1)}, u32[]{:S(2)}, u32[]{:S(2)}) %all-to-all-start.1) | async-done | bytes 8388640 | tf_op jit(solution)/shard_map/all_to_all | solution.py:43
  169.0 7.4 %multiply_reduce_fusion = (f32[256]{0:T(256)S(1)}, f32[2048,256]{1,0:T(8,128)S(1)}) fusion(f32[2048]{0:T(1024)S(1)} %div.40, bf16[2048,2048]{1,0:T(8,128)(2,1)} %bitcast.3, bf16[2048,256]{1,0:T(8,128)(2,1)S(1)} %bitcast.36), kind=kOutput, calls=%fused_computation.5 | convolution fusion | flops 2151677696 | bytes 11543552 | tf_op jit(solution)/shard_map/dot_general | solution.py:50
  176.3 1.9 multiply_reduce_fusion.1
  178.5 0.9 reshape.114
  179.4 11.9 %all-to-all-start.3 = ((f32[32,1,1024]{2,1,0:T(1,128)}), f32[32,1,1024]{2,1,0:T(1,128)S(1)}, u32[]{:S(2)}, u32[]{:S(2)}) async-start(f32[32,1,1024]{2,1,0:T(1,128)} %reshape.114), calls=%async_computation.3 | async-start | bytes 262144 | tf_op jit(solution)/shard_map/all_to_all | solution.py:22
  191.4 7.7 %all-to-all-done.3 = f32[32,1,1024]{2,1,0:T(1,128)S(1)} async-done(((f32[32,1,1024]{2,1,0:T(1,128)}), f32[32,1,1024]{2,1,0:T(1,128)S(1)}, u32[]{:S(2)}, u32[]{:S(2)}) %all-to-all-start.3) | async-done | bytes 131104 | tf_op jit(solution)/shard_map/all_to_all | solution.py:22
  199.0 0.5 broadcast.90
  199.5 0.9 reduce.8
  200.8 0.8 reshape.116
  201.6 13.0 %all-to-all-start.4 = ((f32[16,1,1024]{2,1,0:T(1,128)}), f32[16,1,1024]{2,1,0:T(1,128)S(1)}, u32[]{:S(2)}, u32[]{:S(2)}) async-start(f32[16,1,1024]{2,1,0:T(1,128)} %reshape.116), calls=%async_computation.4 | async-start | bytes 131072 | tf_op jit(solution)/shard_map/all_to_all | solution.py:22
  214.6 0.8 multiply_multiply_fusion
  215.4 10.8 %all-to-all-done.4 = f32[16,1,1024]{2,1,0:T(1,128)S(1)} async-done(((f32[16,1,1024]{2,1,0:T(1,128)}), f32[16,1,1024]{2,1,0:T(1,128)S(1)}, u32[]{:S(2)}, u32[]{:S(2)}) %all-to-all-start.4) | async-done | bytes 65568 | tf_op jit(solution)/shard_map/all_to_all | solution.py:22
  226.2 0.8 reduce.9
  227.3 0.2 fusion.12
  227.5 0.3 convolution_add_fusion
  227.8 1.7 fusion.1
  229.6 5.7 %convolution_bitcast_fusion = f32[32,16,8,128]{3,2,1,0:T(8,128)S(1)} fusion(bf16[2048,256]{1,0:T(8,128)(2,1)S(1)} %fusion.1, bf16[2048,2048]{1,0:T(8,128)(2,1)} %bitcast.3), kind=kOutput, calls=%fused_computation.8 | convolution fusion | flops 2147483648 | bytes 11534336 | tf_op jit(solution)/shard_map/dot_general | solution.py:90
  235.3 0.2 copy.36
  235.5 31.3 %all_to_all.59 = f32[16,128,256]{1,2,0:T(8,128)S(1)} all-to-all(f32[16,128,256]{1,2,0:T(8,128)S(1)} %bitcast.32), channel_id=1, replica_groups=mesh['xl'=2,'y'=4,'c'=2,'z'=16,'xh'=2] {'xl','y','c'}, dimensions={0} | all-to-all | bytes 4194304 | tf_op jit(solution)/shard_map/all_to_all | solution.py:93
  266.9 1.8 copy.33
  (21 shorter events, 1.4 us)
Async XLA Ops:
  3.5 16.0 %all-to-all-start = ((s32[16,2,18]{2,1,0:T(2,128)}), s32[16,2,18]{2,1,0:T(2,128)S(1)}, u32[]{:S(2)}, u32[]{:S(2)}) async-start(s32[16,2,18]{2,1,0:T(2,128)} %broadcast_in_dim.12), calls=%async_computation | async-start | bytes 32768 | tf_op jit(solution)/shard_map/all_to_all | solution.py:22
  13.6 24.1 %copy-start = (bf16[128,2048]{1,0:T(8,128)(2,1)S(1)}, bf16[128,2048]{1,0:T(8,128)(2,1)}, u32[]{:S(2)}) copy-start(bf16[128,2048]{1,0:T(8,128)(2,1)} %param.7) | copy-start | bytes 1572868
  42.0 127.0 %all-to-all-start.1 = ((bf16[16,128,2048]{2,1,0:T(8,128)(2,1)}), bf16[16,128,2048]{2,1,0:T(8,128)(2,1)}, u32[]{:S(2)}, u32[]{:S(2)}) async-start(bf16[16,128,2048]{2,1,0:T(8,128)(2,1)} %stack.2), calls=%async_computation.1 | async-start | bytes 16777216 | tf_op jit(solution)/shard_map/all_to_all | solution.py:43
  178.4 48.7 %copy-start.2 = (s32[32]{0:T(128)S(1)}, s32[32]{0:T(128)}, u32[]{:S(2)}) copy-start(s32[32]{0:T(128)} %param.11) | copy-start | bytes 388
  179.4 19.6 %all-to-all-start.3 = ((f32[32,1,1024]{2,1,0:T(1,128)}), f32[32,1,1024]{2,1,0:T(1,128)S(1)}, u32[]{:S(2)}, u32[]{:S(2)}) async-start(f32[32,1,1024]{2,1,0:T(1,128)} %reshape.114), calls=%async_computation.3 | async-start | bytes 262144 | tf_op jit(solution)/shard_map/all_to_all | solution.py:22
  201.6 24.6 %all-to-all-start.4 = ((f32[16,1,1024]{2,1,0:T(1,128)}), f32[16,1,1024]{2,1,0:T(1,128)S(1)}, u32[]{:S(2)}, u32[]{:S(2)}) async-start(f32[16,1,1024]{2,1,0:T(1,128)} %reshape.116), calls=%async_computation.4 | async-start | bytes 131072 | tf_op jit(solution)/shard_map/all_to_all | solution.py:22
  227.1 8.2 %copy-start.1 = (f32[32,32]{1,0:T(8,128)}, f32[32,32]{1,0:T(8,128)S(1)}, u32[]{:S(2)}) copy-start(f32[32,32]{1,0:T(8,128)S(1)} %reduce_sum.75) | copy-start | bytes 12292
